TPU v7x, 128 devices: a whole 4x4x4 slice. The times are simulated.
128 devices in a mesh: seq: 8 (over z, core), exp: 16 (over y, x).
Axes of the slice: x: 4, y: 4, z: 4, core: 2. Of those that a mesh axis runs over, the one named last changes fastest.
Arguments:
- attn_query: bfloat16 [2048, 6144], P('seq', 'exp'), may hold values from -6 to 6
- attn_key: bfloat16 [2048, 6144], P('seq', 'exp'), may hold values from -6 to 6
- attn_value: bfloat16 [2048, 6144], P('seq', 'exp'), may hold values from -40 to 40
- log_decay: float32 [48, 2048], P('exp', 'seq'), may hold values from -1.5 to 0
- residual: bfloat16 [2048, 6144], P('seq', 'exp'), may hold values from -6 to 6
- norm_gain: bfloat16 [6144], P('exp'), may hold values from 0.099609375 to 1.8984375
- expert_ids: int32 [2048, 2], P('seq'), may hold values from 0 to 15, as said below
- router_weight: bfloat16 [6144, 16], P(None, 'seq'), may hold values from -0.078125 to 0.078125
- gate_weight: bfloat16 [16, 6144, 4608], P('seq', None, 'exp'), may hold values from -0.078125 to 0.078125
- up_weight: bfloat16 [16, 6144, 4608], P('seq', None, 'exp'), may hold values from -0.078125 to 0.078125
- down_weight: bfloat16 [16, 4608, 6144], P('seq', 'exp'), may hold values from -0.125 to 0.125
Outputs:
- layer_out: bfloat16 [2048, 6144], P('seq', 'exp')
Inputs may be any that keep to these rules, and one draw needn't show every extreme that they name: `expert_ids`: each row names two different experts. In every section of 256 consecutive rows no expert is named more than 64 times, and in every section some experts are named exactly 64 times.
All inputs are finite; a program needn't handle non-finite values.
Results may differ from a plain program's by a relative error of at most 0.017.
Values may be sent and summed in bfloat16 or wider, within the bound.
A program may use at most 192 MiB of HBM per device.

v0:
```python
import jax
import jax.numpy as jnp
from jax import lax
from jax.sharding import PartitionSpec as P


def shifted(array, axis, by):
    count = lax.axis_size(axis)
    pairs = [(i, i + by) for i in range(count) if 0 <= i + by < count]
    return lax.ppermute(array, axis, pairs)


def on_device(
    attn_query,
    attn_key,
    attn_value,
    log_decay,
    residual,
    norm_gain,
    expert_ids,
    router_weight,
    gate_weight,
    up_weight,
    down_weight,
):
    heads_here = log_decay.shape[0]
    length = log_decay.shape[1]
    head_size = attn_query.shape[1] // heads_here
    query_rows = attn_query.reshape(length, heads_here, head_size)
    key_rows = attn_key.reshape(length, heads_here, head_size)
    value_rows = attn_value.reshape(length, heads_here, head_size)
    cumulative = jnp.cumsum(log_decay, axis=1)
    causal = lax.broadcasted_iota(jnp.int32, (length, length), 0) >= lax.broadcasted_iota(
        jnp.int32, (length, length), 1
    )
    decay_gap = jnp.where(causal[None], cumulative[:, :, None] - cumulative[:, None, :], 0.0)
    decay_mask = jnp.where(causal[None], jnp.exp(decay_gap), 0.0)
    scores = jnp.einsum("thd,shd->hts", query_rows, key_rows, preferred_element_type=jnp.float32)
    weights = (scores * decay_mask).astype(jnp.bfloat16)
    intra_part = jnp.einsum("hts,shd->thd", weights, value_rows, preferred_element_type=jnp.float32)
    key_fade = jnp.exp(cumulative[:, -1:] - cumulative)
    scaled = (key_fade.T[:, :, None] * key_rows.astype(jnp.float32)).astype(jnp.bfloat16)
    local_state = jnp.einsum("shd,she->hde", scaled, value_rows, preferred_element_type=jnp.float32)
    section_fade = jnp.exp(cumulative[:, -1])
    incoming = jnp.zeros_like(local_state)
    for repeat_index in range(lax.axis_size("seq") - 1):
        incoming = shifted(section_fade[:, None, None] * incoming + local_state, "seq", 1)
    inter_part = jnp.einsum(
        "thd,hde->the", query_rows.astype(jnp.float32), incoming, precision=lax.Precision.HIGHEST
    )
    attn_out = intra_part + jnp.exp(cumulative).T[:, :, None] * inter_part
    mean_square = jnp.mean(attn_out * attn_out, axis=2, keepdims=True)
    normed = (attn_out / jnp.sqrt(mean_square + 1e-06)).reshape(length, heads_here * head_size)
    stream = (residual.astype(jnp.float32) + norm_gain.astype(jnp.float32) * normed).astype(
        jnp.bfloat16
    )
    experts_here = router_weight.shape[1]
    groups = lax.axis_size("seq")
    expert_count = experts_here * groups
    capacity = 4 * length // expert_count
    features = stream.shape[1]
    choices_per_token = expert_ids.shape[1]
    flat_ids = expert_ids.reshape(-1)
    expert_iota = lax.broadcasted_iota(jnp.int32, (1, expert_count), 1)
    onehot = (flat_ids[:, None] == expert_iota).astype(jnp.int32)
    running = jnp.cumsum(onehot, axis=0)
    slot_index = jnp.sum(running * onehot, axis=1) - 1
    target = flat_ids * capacity + slot_index
    place_iota = lax.broadcasted_iota(jnp.int32, (expert_count * capacity, 1), 0)
    route_matrix = (
        (place_iota == target[None, :])
        .astype(jnp.bfloat16)
        .reshape(expert_count * capacity, length, choices_per_token)
        .sum(axis=2)
    )
    outgoing = jnp.dot(route_matrix, stream, preferred_element_type=jnp.float32).astype(
        jnp.bfloat16
    )
    outgoing = outgoing.reshape(groups, experts_here, capacity, features)
    portion = lax.all_gather(
        lax.all_to_all(outgoing, "seq", split_axis=0, concat_axis=0, tiled=True),
        "exp",
        axis=3,
        tiled=True,
    )
    gate_acc = jnp.einsum(
        "sjcd,jdf->sjcf", portion, gate_weight, preferred_element_type=jnp.float32
    )
    upward = jnp.einsum("sjcd,jdf->sjcf", portion, up_weight, preferred_element_type=jnp.float32)
    logits = jnp.einsum("sjcd,dj->sjc", portion, router_weight, preferred_element_type=jnp.float32)
    hidden_act = (jax.nn.silu(gate_acc) * upward).astype(jnp.bfloat16)
    expert_out = lax.psum_scatter(
        jnp.einsum(
            "sjcf,jfd->dsjc", hidden_act, down_weight, preferred_element_type=jnp.float32
        ).astype(jnp.bfloat16),
        "exp",
        scatter_dimension=0,
        tiled=True,
    ).astype(jnp.float32)
    routed = (jax.nn.sigmoid(logits)[None] * expert_out).astype(jnp.bfloat16)
    returned = lax.all_to_all(routed, "seq", split_axis=1, concat_axis=1, tiled=True)
    returned = returned.reshape(features, expert_count * capacity)
    combined = lax.dot_general(
        route_matrix, returned, (((0,), (1,)), ((), ())), preferred_element_type=jnp.float32
    )
    return (stream.astype(jnp.float32) + combined).astype(jnp.bfloat16)


def solution(mesh):
    in_specs = (
        P("seq", "exp"),
        P("seq", "exp"),
        P("seq", "exp"),
        P("exp", "seq"),
        P("seq", "exp"),
        P("exp"),
        P("seq", None),
        P(None, "seq"),
        P("seq", None, "exp"),
        P("seq", None, "exp"),
        P("seq", "exp", None),
    )
    out_specs = P("seq", "exp")
    return jax.shard_map(
        on_device, mesh=mesh, in_specs=in_specs, out_specs=out_specs, check_vma=False
    )
```

profile of v0, /device:TPU:1, one launch (start us, length us, event | category | flops | bytes accessed | tf_op | source)
XLA Modules:
  0.0 400.8 jit_solution(6427846024970069958)
XLA Ops:
  11.2 4.9 %collective-permute-start = (f32[3,128,128]{2,1,0:T(8,128)S(1)}, f32[3,128,128]{2,1,0:T(8,128)S(1)}, u32[]{:S(2)}, u32[]{:S(2)}) collective-permute-start(f32[3,128,128]{2,1,0:T(8,128)S(1)} %get-tuple-element.9), channel_id=1, source_target_pairs={{0,16},{16,32},{32,48},{48,64},{64,80},{80,96},{96,112},{1,17},{17... | collective-permute-start | bytes 589832 | tf_op jit(solution)/shard_map/ppermute | solution.py:10
  18.8 4.4 %collective-permute-start.1 = (f32[3,128,128]{2,1,0:T(8,128)S(1)}, f32[3,128,128]{2,1,0:T(8,128)S(1)}, u32[]{:S(2)}, u32[]{:S(2)}) collective-permute-start(f32[3,128,128]{2,1,0:T(8,128)S(1)} %multiply_add_fusion.5), channel_id=1, source_target_pairs={{0,16},{16,32},{32,48},{48,64},{64,80},{80,96},{96,112},{1,17},{17... | collective-permute-start | bytes 589832 | tf_op jit(solution)/shard_map/ppermute | solution.py:10
  24.4 1.4 collective-permute-done.1
  25.9 4.4 %collective-permute-start.2 = (f32[3,128,128]{2,1,0:T(8,128)S(1)}, f32[3,128,128]{2,1,0:T(8,128)S(1)}, u32[]{:S(2)}, u32[]{:S(2)}) collective-permute-start(f32[3,128,128]{2,1,0:T(8,128)S(1)} %multiply_add_fusion.4), channel_id=1, source_target_pairs={{0,16},{16,32},{32,48},{48,64},{64,80},{80,96},{96,112},{1,17},{17... | collective-permute-start | bytes 589832 | tf_op jit(solution)/shard_map/ppermute | solution.py:10
  30.7 2.2 collective-permute-done.2
  33.0 4.4 %collective-permute-start.3 = (f32[3,128,128]{2,1,0:T(8,128)S(1)}, f32[3,128,128]{2,1,0:T(8,128)S(1)}, u32[]{:S(2)}, u32[]{:S(2)}) collective-permute-start(f32[3,128,128]{2,1,0:T(8,128)S(1)} %multiply_add_fusion.3), channel_id=1, source_target_pairs={{0,16},{16,32},{32,48},{48,64},{64,80},{80,96},{96,112},{1,17},{17... | collective-permute-start | bytes 589832 | tf_op jit(solution)/shard_map/ppermute | solution.py:10
  38.7 1.3 collective-permute-done.3
  40.1 4.4 %collective-permute-start.4 = (f32[3,128,128]{2,1,0:T(8,128)S(1)}, f32[3,128,128]{2,1,0:T(8,128)S(1)}, u32[]{:S(2)}, u32[]{:S(2)}) collective-permute-start(f32[3,128,128]{2,1,0:T(8,128)S(1)} %multiply_add_fusion.2), channel_id=1, source_target_pairs={{0,16},{16,32},{32,48},{48,64},{64,80},{80,96},{96,112},{1,17},{17... | collective-permute-start | bytes 589832 | tf_op jit(solution)/shard_map/ppermute | solution.py:10
  45.2 1.9 collective-permute-done.4
  47.1 4.4 %collective-permute-start.5 = (f32[3,128,128]{2,1,0:T(8,128)S(1)}, f32[3,128,128]{2,1,0:T(8,128)S(1)}, u32[]{:S(2)}, u32[]{:S(2)}) collective-permute-start(f32[3,128,128]{2,1,0:T(8,128)S(1)} %multiply_add_fusion.1), channel_id=1, source_target_pairs={{0,16},{16,32},{32,48},{48,64},{64,80},{80,96},{96,112},{1,17},{17... | collective-permute-start | bytes 589832 | tf_op jit(solution)/shard_map/ppermute | solution.py:10
  52.0 2.1 collective-permute-done.5
  54.2 4.4 %collective-permute-start.6 = (f32[3,128,128]{2,1,0:T(8,128)S(1)}, f32[3,128,128]{2,1,0:T(8,128)S(1)}, u32[]{:S(2)}, u32[]{:S(2)}) collective-permute-start(f32[3,128,128]{2,1,0:T(8,128)S(1)} %multiply_add_fusion), channel_id=1, source_target_pairs={{0,16},{16,32},{32,48},{48,64},{64,80},{80,96},{96,112},{1,17},{17... | collective-permute-start | bytes 589832 | tf_op jit(solution)/shard_map/ppermute | solution.py:10
  59.1 2.1 collective-permute-done.6
  62.4 18.3 %all_to_all.10 = bf16[8,2,64,384]{3,2,1,0:T(8,128)(2,1)S(1)} all-to-all(bf16[8,2,64,384]{3,2,1,0:T(8,128)(2,1)S(1)} %bitcast.110), channel_id=1, replica_groups=mesh['seq'=8,'exp'=16] {'seq'}, dimensions={0} | all-to-all | bytes 1572864 | tf_op jit(solution)/shard_map/all_to_all | solution.py:81
  81.9 98.5 %all-gather.2.cloned.1.call-done = bf16[8,2,64,6144]{3,2,0,1:T(8,128)(2,1)} async-done(((bf16[8,2,64,384]{3,2,0,1:T(8,128)(2,1)}), bf16[8,2,64,6144]{3,2,0,1:T(8,128)(2,1)}) %all-gather.2.cloned.1.call-update) | async-done | bytes 12582928 | tf_op jit(solution)/shard_map/all_gather | solution.py:80
  180.3 11.8 %fusion.3 = f32[2,8,64,288]{3,2,1,0:T(8,128)S(1)} fusion(bf16[8,2,64,6144]{3,2,0,1:T(8,128)(2,1)} %all-gather.2.cloned.1.call-done, bf16[2,6144,288]{1,2,0:T(8,128)(2,1)} %param.19), kind=kOutput, calls=%fused_computation.4 | convolution fusion | flops 3623878656 | bytes 20840448 | tf_op jit(solution)/shard_map/sjcd,jdf->sjcf/dot_general | solution.py:86
  192.1 8.9 %fusion.6 = bf16[8,2,64,288]{3,2,0,1:T(8,128)(2,1)S(1)} fusion(f32[2,8,64,288]{3,2,1,0:T(8,128)S(1)} %fusion.3, bf16[8,2,64,6144]{3,2,0,1:T(8,128)(2,1)S(1)} %copy-done.1, bf16[2,6144,288]{1,2,0:T(8,128)(2,1)} %param.20), kind=kOutput, calls=%fused_computation.9 | convolution fusion | flops 3625648128 | bytes 21430272 | tf_op jit(solution)/shard_map/sjcd,jdf->sjcf/dot_general | solution.py:89
  201.1 12.6 %convert_bitcast_fusion = bf16[6144,8,2,64]{0,3,1,2:T(8,128)(2,1)} fusion(bf16[8,2,64,288]{3,2,0,1:T(8,128)(2,1)S(1)} %fusion.6, bf16[2,288,6144]{2,1,0:T(8,128)(2,1)} %param.21), kind=kOutput, calls=%fused_computation | convolution fusion | flops 3630170112 | bytes 20250624 | tf_op jit(solution)/shard_map/sjcf,jfd->dsjc/dot_general | solution.py:93
  213.7 29.7 %copy.107 = bf16[6144,8,2,64]{3,1,2,0:T(8,128)(2,1)} copy(bf16[6144,8,2,64]{0,3,1,2:T(8,128)(2,1)} %convert_bitcast_fusion) | data formatting | bytes 25165824
  243.4 33.4 %reshape.128 = bf16[6144,1024]{1,0:T(8,128)(2,1)} reshape(bf16[6144,2,8,64]{3,2,1,0:T(8,128)(2,1)} %bitcast.108) | data formatting | bytes 25165824
  276.8 7.9 %fusion.29 = f32[2,1,8,64]{3,1,2,0:T(1,128)S(1)} fusion(bf16[8,2,64,6144]{3,2,0,1:T(8,128)(2,1)} %all-gather.2.cloned.1.call-done, bf16[6144,2,1,1]{0,1,2,3:T(2,128)(2,1)S(1)} %bitcast.107), kind=kOutput, calls=%fused_computation.49 | convolution fusion | flops 12582912 | bytes 12611584 | tf_op jit(solution)/shard_map/sjcd,dj->sjc/dot_general | solution.py:90
  284.7 86.8 %reduce-scatter.4.cloned.1.call-done = bf16[384,1024]{1,0:T(8,128)(2,1)} async-done(((bf16[6144,1024]{1,0:T(8,128)(2,1)}), bf16[384,1024]{1,0:T(8,128)(2,1)}) %reduce-scatter.4.cloned.1.call-update) | async-done | bytes 786448
  371.5 2.5 reshape.129
  375.5 17.3 %all_to_all.11 = bf16[384,8,2,64]{0,3,2,1:T(8,128)(2,1)S(1)} all-to-all(bf16[384,8,2,64]{0,3,2,1:T(8,128)(2,1)S(1)} %copy.96), channel_id=1, replica_groups=mesh['seq'=8,'exp'=16] {'seq'}, dimensions={1} | all-to-all | bytes 1572864 | tf_op jit(solution)/shard_map/all_to_all | solution.py:101
  (63 shorter events, 17.2 us)
Async XLA Ops:
  6.5 270.3 %copy-start = (bf16[6144,2]{0,1:T(2,128)(2,1)S(1)}, bf16[6144,2]{0,1:T(2,128)(2,1)}, u32[]{:S(2)}) copy-start(bf16[6144,2]{0,1:T(2,128)(2,1)} %param.18) | copy-start | bytes 73732
  6.5 55.3 %copy-start.2 = (bf16[256,384]{1,0:T(8,128)(2,1)S(1)}, bf16[256,384]{1,0:T(8,128)(2,1)}, u32[]{:S(2)}) copy-start(bf16[256,384]{1,0:T(8,128)(2,1)} %param.15) | copy-start | bytes 589828
  6.5 173.8 %all-gather.2.cloned.1.call-start = ((), (), s32[]{:S(2)}) async-start(), calls=%async_computation.3 | async-start | bytes 13369344 | tf_op jit(solution)/shard_map/all_gather | solution.py:80
  11.2 7.5 %collective-permute-start = (f32[3,128,128]{2,1,0:T(8,128)S(1)}, f32[3,128,128]{2,1,0:T(8,128)S(1)}, u32[]{:S(2)}, u32[]{:S(2)}) collective-permute-start(f32[3,128,128]{2,1,0:T(8,128)S(1)} %get-tuple-element.9), channel_id=1, source_target_pairs={{0,16},{16,32},{32,48},{48,64},{64,80},{80,96},{96,112},{1,17},{17... | collective-permute-start | bytes 589832 | tf_op jit(solution)/shard_map/ppermute | solution.py:10
  18.8 7.0 %collective-permute-start.1 = (f32[3,128,128]{2,1,0:T(8,128)S(1)}, f32[3,128,128]{2,1,0:T(8,128)S(1)}, u32[]{:S(2)}, u32[]{:S(2)}) collective-permute-start(f32[3,128,128]{2,1,0:T(8,128)S(1)} %multiply_add_fusion.5), channel_id=1, source_target_pairs={{0,16},{16,32},{32,48},{48,64},{64,80},{80,96},{96,112},{1,17},{17... | collective-permute-start | bytes 589832 | tf_op jit(solution)/shard_map/ppermute | solution.py:10
  25.9 7.0 %collective-permute-start.2 = (f32[3,128,128]{2,1,0:T(8,128)S(1)}, f32[3,128,128]{2,1,0:T(8,128)S(1)}, u32[]{:S(2)}, u32[]{:S(2)}) collective-permute-start(f32[3,128,128]{2,1,0:T(8,128)S(1)} %multiply_add_fusion.4), channel_id=1, source_target_pairs={{0,16},{16,32},{32,48},{48,64},{64,80},{80,96},{96,112},{1,17},{17... | collective-permute-start | bytes 589832 | tf_op jit(solution)/shard_map/ppermute | solution.py:10
  33.0 7.0 %collective-permute-start.3 = (f32[3,128,128]{2,1,0:T(8,128)S(1)}, f32[3,128,128]{2,1,0:T(8,128)S(1)}, u32[]{:S(2)}, u32[]{:S(2)}) collective-permute-start(f32[3,128,128]{2,1,0:T(8,128)S(1)} %multiply_add_fusion.3), channel_id=1, source_target_pairs={{0,16},{16,32},{32,48},{48,64},{64,80},{80,96},{96,112},{1,17},{17... | collective-permute-start | bytes 589832 | tf_op jit(solution)/shard_map/ppermute | solution.py:10
  40.1 7.0 %collective-permute-start.4 = (f32[3,128,128]{2,1,0:T(8,128)S(1)}, f32[3,128,128]{2,1,0:T(8,128)S(1)}, u32[]{:S(2)}, u32[]{:S(2)}) collective-permute-start(f32[3,128,128]{2,1,0:T(8,128)S(1)} %multiply_add_fusion.2), channel_id=1, source_target_pairs={{0,16},{16,32},{32,48},{48,64},{64,80},{80,96},{96,112},{1,17},{17... | collective-permute-start | bytes 589832 | tf_op jit(solution)/shard_map/ppermute | solution.py:10
  47.1 7.0 %collective-permute-start.5 = (f32[3,128,128]{2,1,0:T(8,128)S(1)}, f32[3,128,128]{2,1,0:T(8,128)S(1)}, u32[]{:S(2)}, u32[]{:S(2)}) collective-permute-start(f32[3,128,128]{2,1,0:T(8,128)S(1)} %multiply_add_fusion.1), channel_id=1, source_target_pairs={{0,16},{16,32},{32,48},{48,64},{64,80},{80,96},{96,112},{1,17},{17... | collective-permute-start | bytes 589832 | tf_op jit(solution)/shard_map/ppermute | solution.py:10
  54.2 7.0 %collective-permute-start.6 = (f32[3,128,128]{2,1,0:T(8,128)S(1)}, f32[3,128,128]{2,1,0:T(8,128)S(1)}, u32[]{:S(2)}, u32[]{:S(2)}) collective-permute-start(f32[3,128,128]{2,1,0:T(8,128)S(1)} %multiply_add_fusion), channel_id=1, source_target_pairs={{0,16},{16,32},{32,48},{48,64},{64,80},{80,96},{96,112},{1,17},{17... | collective-permute-start | bytes 589832 | tf_op jit(solution)/shard_map/ppermute | solution.py:10
  81.6 289.9 %reduce-scatter.4.cloned.1.call-start = ((), (), s32[]{:S(2)}) async-start(), calls=%async_computation.4 | async-start | bytes 13369344
  180.3 11.8 %copy-start.1 = (bf16[8,2,64,6144]{3,2,0,1:T(8,128)(2,1)S(1)}, bf16[8,2,64,6144]{3,2,0,1:T(8,128)(2,1)}, u32[]{:S(2)}) copy-start(bf16[8,2,64,6144]{3,2,0,1:T(8,128)(2,1)} %all-gather.2.cloned.1.call-done) | copy-start | bytes 37748740
Sparse Core Ops, SparseCore 0:
  81.7 98.5 all-gather.1
  276.9 94.5 reduce-scatter.3
where the time goes:
time: 403 us; the launch traced here: 401 us
  waiting for transfers between devices  197 us (49%)
  local copies, waits for them, and re-layouts  73.9 us (18%)
  matrix products  43.9 us (11%)
  blocking collectives  35.6 us (9%)
  starting transfers between devices  31.5 us (8%)
  between operations  13.7 us (3%)
  other arithmetic  5.1 us (1%)
    all_gather x1, waiting for transfers between devices, on_device(): lax.all_gather(lax.all_to_all(outgoing, 'seq', split_axis=0, concat_axis=...  98.5 us
    unnamed x3, waiting for transfers between devices  86.8 us
    unnamed x16, local copies, waits for them, and re-layouts  70.9 us
    ppermute x7, starting transfers between devices, shifted(): return lax.ppermute(array, axis, pairs)  31.3 us
    all_to_all x1, blocking collectives, on_device(): lax.all_to_all(outgoing, 'seq', split_axis=0, concat_axis=0, tiled=True)  18.3 us
    all_to_all x1, blocking collectives, on_device(): lax.all_to_all(routed, 'seq', split_axis=1, concat_axis=1, tiled=True)  17.3 us
    dot_general x1, matrix products, on_device(): jnp.einsum('sjcf,jfd->dsjc', hidden_act, down_weight, preferred_element_t...  12.6 us
    dot_general x1, matrix products, on_device(): jnp.einsum('sjcd,jdf->sjcf', portion, gate_weight, preferred_element_type...  11.8 us
  transfers between devices with their start and end apart: 9, of which 9 were waited for; matrix products, arithmetic and copies ran while one was open for 4% of the time, Pallas kernels for 0%

commit v1 on v0

--- a/solution.py
+++ b/solution.py
@@ -77,12 +77,25 @@
         jnp.bfloat16
     )
     outgoing = outgoing.reshape(groups, experts_here, capacity, features)
-    portion = lax.all_gather(
-        lax.all_to_all(outgoing, "seq", split_axis=0, concat_axis=0, tiled=True),
-        "exp",
-        axis=3,
-        tiled=True,
-    )
+    x = lax.all_to_all(outgoing, "seq", split_axis=0, concat_axis=0, tiled=True)
+    count_2, index, extent = (lax.axis_size("exp"), lax.axis_index("exp"), x.shape[3])
+    right = [(i_2, (i_2 + 1) % count_2) for i_2 in range(count_2)]
+    left = [(i_2, (i_2 - 1) % count_2) for i_2 in range(count_2)]
+    out = jnp.zeros((*x.shape[:3], count_2 * extent, *x.shape[3 + 1 :]), x.dtype)
+    out = lax.dynamic_update_slice_in_dim(out, x, index * extent, axis=3)
+    from_left = from_right = x
+    half = count_2 // 2
+    for lap in range(1, half + 1):
+        from_left = lax.ppermute(from_left, "exp", right)
+        out = lax.dynamic_update_slice_in_dim(
+            out, from_left, (index - lap) % count_2 * extent, axis=3
+        )
+        if lap < count_2 - half:
+            from_right = lax.ppermute(from_right, "exp", left)
+            out = lax.dynamic_update_slice_in_dim(
+                out, from_right, (index + lap) % count_2 * extent, axis=3
+            )
+    portion = out
     gate_acc = jnp.einsum(
         "sjcd,jdf->sjcf", portion, gate_weight, preferred_element_type=jnp.float32
     )

time: 403 us -> 457 us (1.13)
  starting transfers between devices: 31.5 us -> 67.2 us
  local copies, waits for them, and re-layouts: 73.9 us -> 98.2 us
  waiting for transfers between devices: 197 us -> 190 us
    all_gather x1 -> x0, waiting for transfers between devices: 98.5 us -> none  [on_device(): lax.all_gather(lax.all_to_all(outgoing, 'seq', split_axis=0, concat_axis=...]
    ppermute x0 -> x15, waiting for transfers between devices: none -> 87.4 us  [the longest x8 70.5 us: on_device(): from_left = lax.ppermute(from_left, 'exp', right)]
    ppermute x0 -> x15, starting transfers between devices: none -> 36 us  [the longest x7 34.7 us: on_device(): from_right = lax.ppermute(from_right, 'exp', left)]
    dynamic_update_slice x0 -> x16, local copies, waits for them, and re-layouts: none -> 19.1 us  [the longest x8 9.53 us: on_device(): lax.dynamic_update_slice_in_dim(out, from_left, (index - lap) % count_2 *...]
    broadcast_in_dim x0 -> x1, local copies, waits for them, and re-layouts: none -> 6.04 us  [on_device(): out = jnp.zeros((*x.shape[:3], count_2 * extent, *x.shape[3 + 1:]), x.dtype)]
    unnamed x3 -> x2, waiting for transfers between devices: 86.8 us -> 91.1 us
    unnamed x16 -> x22, local copies, waits for them, and re-layouts: 70.9 us -> 71 us
  transfers between devices with their start and end apart: 9 -> 23, of which waited for: 9 -> 20; matrix products, arithmetic and copies ran while one was open for 4% -> 8% of each run, Pallas kernels for 0% -> 0%
where the time goes in v1:
time: 457 us; the launch traced here: 455 us
  waiting for transfers between devices  190 us (42%)
  local copies, waits for them, and re-layouts  98.2 us (21%)
  starting transfers between devices  67.2 us (15%)
  matrix products  44 us (10%)
  blocking collectives  35.6 us (8%)
  between operations  13.7 us (3%)
  other arithmetic  6.04 us (1%)
    unnamed x2, waiting for transfers between devices  91.1 us
    unnamed x22, local copies, waits for them, and re-layouts  71 us
    ppermute x8, waiting for transfers between devices, on_device(): from_left = lax.ppermute(from_left, 'exp', right)  70.5 us
    ppermute x7, starting transfers between devices, on_device(): from_right = lax.ppermute(from_right, 'exp', left)  34.7 us
    ppermute x7, starting transfers between devices, shifted(): return lax.ppermute(array, axis, pairs)  31.3 us
    all_to_all x1, blocking collectives, on_device(): x = lax.all_to_all(outgoing, 'seq', split_axis=0, concat_axis=0, tiled=True)  18.3 us
    all_to_all x1, blocking collectives, on_device(): lax.all_to_all(routed, 'seq', split_axis=1, concat_axis=1, tiled=True)  17.3 us
    ppermute x7, waiting for transfers between devices, on_device(): from_right = lax.ppermute(from_right, 'exp', left)  16.9 us
  transfers between devices with their start and end apart: 23, of which 20 were waited for; matrix products, arithmetic and copies ran while one was open for 8% of the time, Pallas kernels for 0%

profile of v1, /device:TPU:1, one launch (start us, length us, event | category | flops | bytes accessed | tf_op | source)
XLA Modules:
  0.0 455.0 jit_solution(15612553029655314498)
XLA Ops:
  11.2 4.9 %collective-permute-start = (f32[3,128,128]{2,1,0:T(8,128)S(1)}, f32[3,128,128]{2,1,0:T(8,128)S(1)}, u32[]{:S(2)}, u32[]{:S(2)}) collective-permute-start(f32[3,128,128]{2,1,0:T(8,128)S(1)} %get-tuple-element.9), channel_id=1, source_target_pairs={{0,16},{16,32},{32,48},{48,64},{64,80},{80,96},{96,112},{1,17},{17... | collective-permute-start | bytes 589832 | tf_op jit(solution)/shard_map/ppermute | solution.py:10
  63.2 18.3 %all_to_all.10 = bf16[8,2,64,384]{3,2,1,0:T(8,128)(2,1)S(1)} all-to-all(bf16[8,2,64,384]{3,2,1,0:T(8,128)(2,1)S(1)} %bitcast.110), channel_id=1, replica_groups=mesh['seq'=8,'exp'=16] {'seq'}, dimensions={0} | all-to-all | bytes 1572864 | tf_op jit(solution)/shard_map/all_to_all | solution.py:80
  86.5 16.7 %collective-permute-done.7 = bf16[8,2,64,384]{3,2,1,0:T(8,128)(2,1)S(1)} collective-permute-done((bf16[8,2,64,384]{3,2,1,0:T(8,128)(2,1)S(1)}, bf16[8,2,64,384]{3,2,1,0:T(8,128)(2,1)S(1)}, u32[]{:S(2)}, u32[]{:S(2)}) %collective-permute-start.7) | collective-permute-done | bytes 786464 | tf_op jit(solution)/shard_map/ppermute | solution.py:89
  103.2 4.8 %collective-permute-start.10 = (bf16[8,2,64,384]{3,2,1,0:T(8,128)(2,1)S(1)}, bf16[8,2,64,384]{3,2,1,0:T(8,128)(2,1)}, u32[]{:S(2)}, u32[]{:S(2)}) collective-permute-start(bf16[8,2,64,384]{3,2,1,0:T(8,128)(2,1)S(1)} %collective-permute-done.8), channel_id=1, source_target_pairs={{0,15},{1,0},{2,1},{3,2},{4,3},{5,4},{6,5},{7,6},{8,7},{9,8},{10,9... | collective-permute-start | bytes 2359304 | tf_op jit(solution)/shard_map/ppermute | solution.py:94
  107.9 15.9 %collective-permute-done.9 = bf16[8,2,64,384]{3,2,1,0:T(8,128)(2,1)} collective-permute-done((bf16[8,2,64,384]{3,2,1,0:T(8,128)(2,1)S(1)}, bf16[8,2,64,384]{3,2,1,0:T(8,128)(2,1)}, u32[]{:S(2)}, u32[]{:S(2)}) %collective-permute-start.9) | collective-permute-done | bytes 786464 | tf_op jit(solution)/shard_map/ppermute | solution.py:89
  123.8 4.8 %collective-permute-start.12 = (bf16[8,2,64,384]{3,2,1,0:T(8,128)(2,1)}, bf16[8,2,64,384]{3,2,1,0:T(8,128)(2,1)S(1)}, u32[]{:S(2)}, u32[]{:S(2)}) collective-permute-start(bf16[8,2,64,384]{3,2,1,0:T(8,128)(2,1)} %collective-permute-done.10), channel_id=1, source_target_pairs={{0,15},{1,0},{2,1},{3,2},{4,3},{5,4},{6,5},{7,6},{8,7},{9,8},{10,9... | collective-permute-start | bytes 2359304 | tf_op jit(solution)/shard_map/ppermute | solution.py:94
  128.6 15.0 %collective-permute-done.11 = bf16[8,2,64,384]{3,2,1,0:T(8,128)(2,1)S(1)} collective-permute-done((bf16[8,2,64,384]{3,2,1,0:T(8,128)(2,1)}, bf16[8,2,64,384]{3,2,1,0:T(8,128)(2,1)S(1)}, u32[]{:S(2)}, u32[]{:S(2)}) %collective-permute-start.11) | collective-permute-done | bytes 786464 | tf_op jit(solution)/shard_map/ppermute | solution.py:89
  143.7 6.0 %broadcast_in_dim.25 = bf16[8,2,64,6144]{3,2,0,1:T(8,128)(2,1)} broadcast(bf16[]{:T(256)} %constant.114.clone.1), dimensions={} | broadcast | bytes 12582914 | tf_op jit(solution)/shard_map/broadcast_in_dim | solution.py:84
  151.8 4.9 %collective-permute-start.14 = (bf16[8,2,64,384]{3,2,1,0:T(8,128)(2,1)S(1)}, bf16[8,2,64,384]{3,2,1,0:T(8,128)(2,1)S(1)}, u32[]{:S(2)}, u32[]{:S(2)}) collective-permute-start(bf16[8,2,64,384]{3,2,1,0:T(8,128)(2,1)S(1)} %collective-permute-done.12), channel_id=1, source_target_pairs={{0,15},{1,0},{2,1},{3,2},{4,3},{5,4},{6,5},{7,6},{8,7},{9,8},{10,9... | collective-permute-start | bytes 2359304 | tf_op jit(solution)/shard_map/ppermute | solution.py:94
  169.6 5.5 %collective-permute-start.16 = (bf16[8,2,64,384]{3,2,1,0:T(8,128)(2,1)S(1)}, bf16[8,2,64,384]{3,2,1,0:T(8,128)(2,1)S(1)}, u32[]{:S(2)}, u32[]{:S(2)}) collective-permute-start(bf16[8,2,64,384]{3,2,1,0:T(8,128)(2,1)S(1)} %collective-permute-done.14), channel_id=1, source_target_pairs={{0,15},{1,0},{2,1},{3,2},{4,3},{5,4},{6,5},{7,6},{8,7},{9,8},{10,9... | collective-permute-start | bytes 2359304 | tf_op jit(solution)/shard_map/ppermute | solution.py:94
  182.2 4.9 %collective-permute-done.16 = bf16[8,2,64,384]{3,2,1,0:T(8,128)(2,1)S(1)} collective-permute-done((bf16[8,2,64,384]{3,2,1,0:T(8,128)(2,1)S(1)}, bf16[8,2,64,384]{3,2,1,0:T(8,128)(2,1)S(1)}, u32[]{:S(2)}, u32[]{:S(2)}) %collective-permute-start.16) | collective-permute-done | bytes 786464 | tf_op jit(solution)/shard_map/ppermute | solution.py:94
  187.1 5.5 %collective-permute-start.18 = (bf16[8,2,64,384]{3,2,1,0:T(8,128)(2,1)S(1)}, bf16[8,2,64,384]{3,2,1,0:T(8,128)(2,1)S(1)}, u32[]{:S(2)}, u32[]{:S(2)}) collective-permute-start(bf16[8,2,64,384]{3,2,1,0:T(8,128)(2,1)S(1)} %collective-permute-done.16), channel_id=1, source_target_pairs={{0,15},{1,0},{2,1},{3,2},{4,3},{5,4},{6,5},{7,6},{8,7},{9,8},{10,9... | collective-permute-start | bytes 2359304 | tf_op jit(solution)/shard_map/ppermute | solution.py:94
  199.1 4.6 %collective-permute-done.18 = bf16[8,2,64,384]{3,2,1,0:T(8,128)(2,1)S(1)} collective-permute-done((bf16[8,2,64,384]{3,2,1,0:T(8,128)(2,1)S(1)}, bf16[8,2,64,384]{3,2,1,0:T(8,128)(2,1)S(1)}, u32[]{:S(2)}, u32[]{:S(2)}) %collective-permute-start.18) | collective-permute-done | bytes 786464 | tf_op jit(solution)/shard_map/ppermute | solution.py:94
  203.7 5.5 %collective-permute-start.20 = (bf16[8,2,64,384]{3,2,1,0:T(8,128)(2,1)S(1)}, bf16[8,2,64,384]{3,2,1,0:T(8,128)(2,1)S(1)}, u32[]{:S(2)}, u32[]{:S(2)}) collective-permute-start(bf16[8,2,64,384]{3,2,1,0:T(8,128)(2,1)S(1)} %collective-permute-done.18), channel_id=1, source_target_pairs={{0,15},{1,0},{2,1},{3,2},{4,3},{5,4},{6,5},{7,6},{8,7},{9,8},{10,9... | collective-permute-start | bytes 2359304 | tf_op jit(solution)/shard_map/ppermute | solution.py:94
  215.1 4.6 %collective-permute-done.20 = bf16[8,2,64,384]{3,2,1,0:T(8,128)(2,1)S(1)} collective-permute-done((bf16[8,2,64,384]{3,2,1,0:T(8,128)(2,1)S(1)}, bf16[8,2,64,384]{3,2,1,0:T(8,128)(2,1)S(1)}, u32[]{:S(2)}, u32[]{:S(2)}) %collective-permute-start.20) | collective-permute-done | bytes 786464 | tf_op jit(solution)/shard_map/ppermute | solution.py:94
  220.7 8.2 %collective-permute-done.21 = bf16[8,2,64,384]{3,2,1,0:T(8,128)(2,1)S(1)} collective-permute-done((bf16[8,2,64,384]{3,2,1,0:T(8,128)(2,1)S(1)}, bf16[8,2,64,384]{3,2,1,0:T(8,128)(2,1)S(1)}, u32[]{:S(2)}, u32[]{:S(2)}) %collective-permute-start.21) | collective-permute-done | bytes 786464 | tf_op jit(solution)/shard_map/ppermute | solution.py:89
  230.1 11.8 %fusion.3 = f32[2,8,64,288]{3,2,1,0:T(8,128)S(1)} fusion(bf16[8,2,64,6144]{3,2,0,1:T(8,128)(2,1)} %copy_dynamic-update-slice_fusion, bf16[2,6144,288]{1,2,0:T(8,128)(2,1)} %param.19), kind=kOutput, calls=%fused_computation.4 | convolution fusion | flops 3623878656 | bytes 20840448 | tf_op jit(solution)/shard_map/sjcd,jdf->sjcf/dot_general | solution.py:99
  241.9 8.9 %fusion.6 = bf16[8,2,64,288]{3,2,0,1:T(8,128)(2,1)S(1)} fusion(f32[2,8,64,288]{3,2,1,0:T(8,128)S(1)} %fusion.3, bf16[8,2,64,6144]{3,2,0,1:T(8,128)(2,1)S(1)} %copy-done.1, bf16[2,6144,288]{1,2,0:T(8,128)(2,1)} %param.20), kind=kOutput, calls=%fused_computation.9 | convolution fusion | flops 3625648128 | bytes 21430272 | tf_op jit(solution)/shard_map/sjcd,jdf->sjcf/dot_general | solution.py:102
  250.8 12.6 %convert_bitcast_fusion = bf16[6144,8,2,64]{0,3,1,2:T(8,128)(2,1)} fusion(bf16[8,2,64,288]{3,2,0,1:T(8,128)(2,1)S(1)} %fusion.6, bf16[2,288,6144]{2,1,0:T(8,128)(2,1)} %param.21), kind=kOutput, calls=%fused_computation | convolution fusion | flops 3630170112 | bytes 20250624 | tf_op jit(solution)/shard_map/sjcf,jfd->dsjc/dot_general | solution.py:106
  263.4 29.8 %copy.152 = bf16[6144,8,2,64]{3,1,2,0:T(8,128)(2,1)} copy(bf16[6144,8,2,64]{0,3,1,2:T(8,128)(2,1)} %convert_bitcast_fusion) | data formatting | bytes 25165824
  293.2 33.5 %reshape.128 = bf16[6144,1024]{1,0:T(8,128)(2,1)} reshape(bf16[6144,2,8,64]{3,2,1,0:T(8,128)(2,1)} %bitcast.108) | data formatting | bytes 25165824
  326.7 7.9 %fusion.29 = f32[2,1,8,64]{3,1,2,0:T(1,128)S(1)} fusion(bf16[8,2,64,6144]{3,2,0,1:T(8,128)(2,1)} %copy_dynamic-update-slice_fusion, bf16[6144,2,1,1]{0,1,2,3:T(2,128)(2,1)S(1)} %bitcast.107), kind=kOutput, calls=%fused_computation.65 | convolution fusion | flops 12582912 | bytes 12611584 | tf_op jit(solution)/shard_map/sjcd,dj->sjc/dot_general | solution.py:103
  334.6 91.1 %reduce-scatter.4.cloned.1.call-done = bf16[384,1024]{1,0:T(8,128)(2,1)} async-done(((bf16[6144,1024]{1,0:T(8,128)(2,1)}), bf16[384,1024]{1,0:T(8,128)(2,1)}) %reduce-scatter.4.cloned.1.call-update) | async-done | bytes 786448
  429.7 17.3 %all_to_all.11 = bf16[384,8,2,64]{0,3,2,1:T(8,128)(2,1)S(1)} all-to-all(bf16[384,8,2,64]{0,3,2,1:T(8,128)(2,1)S(1)} %copy.141), channel_id=1, replica_groups=mesh['seq'=8,'exp'=16] {'seq'}, dimensions={1} | all-to-all | bytes 1572864 | tf_op jit(solution)/shard_map/all_to_all | solution.py:114
  (112 shorter events, 98.1 us)
Async XLA Ops:
  6.5 320.1 %copy-start = (bf16[6144,2]{0,1:T(2,128)(2,1)S(1)}, bf16[6144,2]{0,1:T(2,128)(2,1)}, u32[]{:S(2)}) copy-start(bf16[6144,2]{0,1:T(2,128)(2,1)} %param.18) | copy-start | bytes 73732
  6.5 419.2 %reduce-scatter.4.cloned.1.call-start = ((), (), s32[]{:S(2)}) async-start(), calls=%async_computation.3 | async-start | bytes 13369344
  11.2 7.5 %collective-permute-start = (f32[3,128,128]{2,1,0:T(8,128)S(1)}, f32[3,128,128]{2,1,0:T(8,128)S(1)}, u32[]{:S(2)}, u32[]{:S(2)}) collective-permute-start(f32[3,128,128]{2,1,0:T(8,128)S(1)} %get-tuple-element.9), channel_id=1, source_target_pairs={{0,16},{16,32},{32,48},{48,64},{64,80},{80,96},{96,112},{1,17},{17... | collective-permute-start | bytes 589832 | tf_op jit(solution)/shard_map/ppermute | solution.py:10
  18.8 7.0 %collective-permute-start.1 = (f32[3,128,128]{2,1,0:T(8,128)S(1)}, f32[3,128,128]{2,1,0:T(8,128)S(1)}, u32[]{:S(2)}, u32[]{:S(2)}) collective-permute-start(f32[3,128,128]{2,1,0:T(8,128)S(1)} %multiply_add_fusion.5), channel_id=1, source_target_pairs={{0,16},{16,32},{32,48},{48,64},{64,80},{80,96},{96,112},{1,17},{17... | collective-permute-start | bytes 589832 | tf_op jit(solution)/shard_map/ppermute | solution.py:10
  25.9 7.0 %collective-permute-start.2 = (f32[3,128,128]{2,1,0:T(8,128)S(1)}, f32[3,128,128]{2,1,0:T(8,128)S(1)}, u32[]{:S(2)}, u32[]{:S(2)}) collective-permute-start(f32[3,128,128]{2,1,0:T(8,128)S(1)} %multiply_add_fusion.4), channel_id=1, source_target_pairs={{0,16},{16,32},{32,48},{48,64},{64,80},{80,96},{96,112},{1,17},{17... | collective-permute-start | bytes 589832 | tf_op jit(solution)/shard_map/ppermute | solution.py:10
  33.0 7.0 %collective-permute-start.3 = (f32[3,128,128]{2,1,0:T(8,128)S(1)}, f32[3,128,128]{2,1,0:T(8,128)S(1)}, u32[]{:S(2)}, u32[]{:S(2)}) collective-permute-start(f32[3,128,128]{2,1,0:T(8,128)S(1)} %multiply_add_fusion.3), channel_id=1, source_target_pairs={{0,16},{16,32},{32,48},{48,64},{64,80},{80,96},{96,112},{1,17},{17... | collective-permute-start | bytes 589832 | tf_op jit(solution)/shard_map/ppermute | solution.py:10
  40.0 7.0 %collective-permute-start.4 = (f32[3,128,128]{2,1,0:T(8,128)S(1)}, f32[3,128,128]{2,1,0:T(8,128)S(1)}, u32[]{:S(2)}, u32[]{:S(2)}) collective-permute-start(f32[3,128,128]{2,1,0:T(8,128)S(1)} %multiply_add_fusion.2), channel_id=1, source_target_pairs={{0,16},{16,32},{32,48},{48,64},{64,80},{80,96},{96,112},{1,17},{17... | collective-permute-start | bytes 589832 | tf_op jit(solution)/shard_map/ppermute | solution.py:10
  47.1 7.0 %collective-permute-start.5 = (f32[3,128,128]{2,1,0:T(8,128)S(1)}, f32[3,128,128]{2,1,0:T(8,128)S(1)}, u32[]{:S(2)}, u32[]{:S(2)}) collective-permute-start(f32[3,128,128]{2,1,0:T(8,128)S(1)} %multiply_add_fusion.1), channel_id=1, source_target_pairs={{0,16},{16,32},{32,48},{48,64},{64,80},{80,96},{96,112},{1,17},{17... | collective-permute-start | bytes 589832 | tf_op jit(solution)/shard_map/ppermute | solution.py:10
  54.2 7.0 %collective-permute-start.6 = (f32[3,128,128]{2,1,0:T(8,128)S(1)}, f32[3,128,128]{2,1,0:T(8,128)S(1)}, u32[]{:S(2)}, u32[]{:S(2)}) collective-permute-start(f32[3,128,128]{2,1,0:T(8,128)S(1)} %multiply_add_fusion), channel_id=1, source_target_pairs={{0,16},{16,32},{32,48},{48,64},{64,80},{80,96},{96,112},{1,17},{17... | collective-permute-start | bytes 589832 | tf_op jit(solution)/shard_map/ppermute | solution.py:10
  81.5 21.6 %collective-permute-start.7 = (bf16[8,2,64,384]{3,2,1,0:T(8,128)(2,1)S(1)}, bf16[8,2,64,384]{3,2,1,0:T(8,128)(2,1)S(1)}, u32[]{:S(2)}, u32[]{:S(2)}) collective-permute-start(bf16[8,2,64,384]{3,2,1,0:T(8,128)(2,1)S(1)} %all_to_all.10), channel_id=1, source_target_pairs={{0,1},{1,2},{2,3},{3,4},{4,5},{5,6},{6,7},{7,8},{8,9},{9,10},{10,1... | collective-permute-start | bytes 2359304 | tf_op jit(solution)/shard_map/ppermute | solution.py:89
  82.7 20.4 %collective-permute-start.8 = (bf16[8,2,64,384]{3,2,1,0:T(8,128)(2,1)S(1)}, bf16[8,2,64,384]{3,2,1,0:T(8,128)(2,1)S(1)}, u32[]{:S(2)}, u32[]{:S(2)}) collective-permute-start(bf16[8,2,64,384]{3,2,1,0:T(8,128)(2,1)S(1)} %all_to_all.10), channel_id=1, source_target_pairs={{0,15},{1,0},{2,1},{3,2},{4,3},{5,4},{6,5},{7,6},{8,7},{9,8},{10,9... | collective-permute-start | bytes 2359304 | tf_op jit(solution)/shard_map/ppermute | solution.py:94
  103.2 20.7 %collective-permute-start.9 = (bf16[8,2,64,384]{3,2,1,0:T(8,128)(2,1)S(1)}, bf16[8,2,64,384]{3,2,1,0:T(8,128)(2,1)}, u32[]{:S(2)}, u32[]{:S(2)}) collective-permute-start(bf16[8,2,64,384]{3,2,1,0:T(8,128)(2,1)S(1)} %collective-permute-done.7), channel_id=1, source_target_pairs={{0,1},{1,2},{2,3},{3,4},{4,5},{5,6},{6,7},{7,8},{8,9},{9,10},{10,1... | collective-permute-start | bytes 2359304 | tf_op jit(solution)/shard_map/ppermute | solution.py:89
  103.2 20.7 %collective-permute-start.10 = (bf16[8,2,64,384]{3,2,1,0:T(8,128)(2,1)S(1)}, bf16[8,2,64,384]{3,2,1,0:T(8,128)(2,1)}, u32[]{:S(2)}, u32[]{:S(2)}) collective-permute-start(bf16[8,2,64,384]{3,2,1,0:T(8,128)(2,1)S(1)} %collective-permute-done.8), channel_id=1, source_target_pairs={{0,15},{1,0},{2,1},{3,2},{4,3},{5,4},{6,5},{7,6},{8,7},{9,8},{10,9... | collective-permute-start | bytes 2359304 | tf_op jit(solution)/shard_map/ppermute | solution.py:94
  123.8 19.8 %collective-permute-start.11 = (bf16[8,2,64,384]{3,2,1,0:T(8,128)(2,1)}, bf16[8,2,64,384]{3,2,1,0:T(8,128)(2,1)S(1)}, u32[]{:S(2)}, u32[]{:S(2)}) collective-permute-start(bf16[8,2,64,384]{3,2,1,0:T(8,128)(2,1)} %collective-permute-done.9), channel_id=1, source_target_pairs={{0,1},{1,2},{2,3},{3,4},{4,5},{5,6},{6,7},{7,8},{8,9},{9,10},{10,1... | collective-permute-start | bytes 2359304 | tf_op jit(solution)/shard_map/ppermute | solution.py:89
  123.8 28.0 %collective-permute-start.12 = (bf16[8,2,64,384]{3,2,1,0:T(8,128)(2,1)}, bf16[8,2,64,384]{3,2,1,0:T(8,128)(2,1)S(1)}, u32[]{:S(2)}, u32[]{:S(2)}) collective-permute-start(bf16[8,2,64,384]{3,2,1,0:T(8,128)(2,1)} %collective-permute-done.10), channel_id=1, source_target_pairs={{0,15},{1,0},{2,1},{3,2},{4,3},{5,4},{6,5},{7,6},{8,7},{9,8},{10,9... | collective-permute-start | bytes 2359304 | tf_op jit(solution)/shard_map/ppermute | solution.py:94
  143.7 18.7 %collective-permute-start.13 = (bf16[8,2,64,384]{3,2,1,0:T(8,128)(2,1)S(1)}, bf16[8,2,64,384]{3,2,1,0:T(8,128)(2,1)S(1)}, u32[]{:S(2)}, u32[]{:S(2)}) collective-permute-start(bf16[8,2,64,384]{3,2,1,0:T(8,128)(2,1)S(1)} %collective-permute-done.11), channel_id=1, source_target_pairs={{0,1},{1,2},{2,3},{3,4},{4,5},{5,6},{6,7},{7,8},{8,9},{9,10},{10,1... | collective-permute-start | bytes 2359304 | tf_op jit(solution)/shard_map/ppermute | solution.py:89
  151.8 17.8 %collective-permute-start.14 = (bf16[8,2,64,384]{3,2,1,0:T(8,128)(2,1)S(1)}, bf16[8,2,64,384]{3,2,1,0:T(8,128)(2,1)S(1)}, u32[]{:S(2)}, u32[]{:S(2)}) collective-permute-start(bf16[8,2,64,384]{3,2,1,0:T(8,128)(2,1)S(1)} %collective-permute-done.12), channel_id=1, source_target_pairs={{0,15},{1,0},{2,1},{3,2},{4,3},{5,4},{6,5},{7,6},{8,7},{9,8},{10,9... | collective-permute-start | bytes 2359304 | tf_op jit(solution)/shard_map/ppermute | solution.py:94
  162.4 17.8 %collective-permute-start.15 = (bf16[8,2,64,384]{3,2,1,0:T(8,128)(2,1)S(1)}, bf16[8,2,64,384]{3,2,1,0:T(8,128)(2,1)S(1)}, u32[]{:S(2)}, u32[]{:S(2)}) collective-permute-start(bf16[8,2,64,384]{3,2,1,0:T(8,128)(2,1)S(1)} %collective-permute-done.13), channel_id=1, source_target_pairs={{0,1},{1,2},{2,3},{3,4},{4,5},{5,6},{6,7},{7,8},{8,9},{9,10},{10,1... | collective-permute-start | bytes 2359304 | tf_op jit(solution)/shard_map/ppermute | solution.py:89
  169.6 17.5 %collective-permute-start.16 = (bf16[8,2,64,384]{3,2,1,0:T(8,128)(2,1)S(1)}, bf16[8,2,64,384]{3,2,1,0:T(8,128)(2,1)S(1)}, u32[]{:S(2)}, u32[]{:S(2)}) collective-permute-start(bf16[8,2,64,384]{3,2,1,0:T(8,128)(2,1)S(1)} %collective-permute-done.14), channel_id=1, source_target_pairs={{0,15},{1,0},{2,1},{3,2},{4,3},{5,4},{6,5},{7,6},{8,7},{9,8},{10,9... | collective-permute-start | bytes 2359304 | tf_op jit(solution)/shard_map/ppermute | solution.py:94
  180.2 16.9 %collective-permute-start.17 = (bf16[8,2,64,384]{3,2,1,0:T(8,128)(2,1)S(1)}, bf16[8,2,64,384]{3,2,1,0:T(8,128)(2,1)S(1)}, u32[]{:S(2)}, u32[]{:S(2)}) collective-permute-start(bf16[8,2,64,384]{3,2,1,0:T(8,128)(2,1)S(1)} %collective-permute-done.15), channel_id=1, source_target_pairs={{0,1},{1,2},{2,3},{3,4},{4,5},{5,6},{6,7},{7,8},{8,9},{9,10},{10,1... | collective-permute-start | bytes 2359304 | tf_op jit(solution)/shard_map/ppermute | solution.py:89
  187.1 16.6 %collective-permute-start.18 = (bf16[8,2,64,384]{3,2,1,0:T(8,128)(2,1)S(1)}, bf16[8,2,64,384]{3,2,1,0:T(8,128)(2,1)S(1)}, u32[]{:S(2)}, u32[]{:S(2)}) collective-permute-start(bf16[8,2,64,384]{3,2,1,0:T(8,128)(2,1)S(1)} %collective-permute-done.16), channel_id=1, source_target_pairs={{0,15},{1,0},{2,1},{3,2},{4,3},{5,4},{6,5},{7,6},{8,7},{9,8},{10,9... | collective-permute-start | bytes 2359304 | tf_op jit(solution)/shard_map/ppermute | solution.py:94
  197.0 15.9 %collective-permute-start.19 = (bf16[8,2,64,384]{3,2,1,0:T(8,128)(2,1)S(1)}, bf16[8,2,64,384]{3,2,1,0:T(8,128)(2,1)S(1)}, u32[]{:S(2)}, u32[]{:S(2)}) collective-permute-start(bf16[8,2,64,384]{3,2,1,0:T(8,128)(2,1)S(1)} %collective-permute-done.17), channel_id=1, source_target_pairs={{0,1},{1,2},{2,3},{3,4},{4,5},{5,6},{6,7},{7,8},{8,9},{9,10},{10,1... | collective-permute-start | bytes 2359304 | tf_op jit(solution)/shard_map/ppermute | solution.py:89
  203.7 16.0 %collective-permute-start.20 = (bf16[8,2,64,384]{3,2,1,0:T(8,128)(2,1)S(1)}, bf16[8,2,64,384]{3,2,1,0:T(8,128)(2,1)S(1)}, u32[]{:S(2)}, u32[]{:S(2)}) collective-permute-start(bf16[8,2,64,384]{3,2,1,0:T(8,128)(2,1)S(1)} %collective-permute-done.18), channel_id=1, source_target_pairs={{0,15},{1,0},{2,1},{3,2},{4,3},{5,4},{6,5},{7,6},{8,7},{9,8},{10,9... | collective-permute-start | bytes 2359304 | tf_op jit(solution)/shard_map/ppermute | solution.py:94
  213.0 16.0 %collective-permute-start.21 = (bf16[8,2,64,384]{3,2,1,0:T(8,128)(2,1)S(1)}, bf16[8,2,64,384]{3,2,1,0:T(8,128)(2,1)S(1)}, u32[]{:S(2)}, u32[]{:S(2)}) collective-permute-start(bf16[8,2,64,384]{3,2,1,0:T(8,128)(2,1)S(1)} %collective-permute-done.19), channel_id=1, source_target_pairs={{0,1},{1,2},{2,3},{3,4},{4,5},{5,6},{6,7},{7,8},{8,9},{9,10},{10,1... | collective-permute-start | bytes 2359304 | tf_op jit(solution)/shard_map/ppermute | solution.py:89
  (5 other events, 87.5 us)
Sparse Core Ops, SparseCore 0:
  326.8 98.8 reduce-scatter.3
